TPU v7x, 32 devices: a whole 2x2x4 slice. The times are simulated.
32 devices in a mesh: dp: 4 (over x, core), ctx: 8 (over z, y).
Axes of the slice: x: 2, y: 2, z: 4, core: 2. Of those that a mesh axis runs over, the one named last changes fastest.
Arguments:
- query: bfloat16 [4, 1024, 2048], P('dp', 'ctx'), may hold values from -6 to 6
- keys: bfloat16 [4, 1024, 2048], P('dp', 'ctx'), may hold values from -6 to 6
- values: bfloat16 [4, 1024, 2048], P('dp', 'ctx'), may hold values from -6 to 6
- cotangent: bfloat16 [4, 1024, 2048], P('dp', 'ctx'), may hold values from -6 to 6
- long_filter: bfloat16 [1024, 2048], P('ctx'), may hold values from -1.05 to 1.05, as said below
- short_weights: float32 [3, 3, 2048], replicated, may hold values from -3 to 3
- skip: float32 [2048], replicated, may hold values from -4 to 4
- lengths: int32 [4, 16], P('dp'), may hold values from 1 to 256, 1024 in all within a row
Outputs:
- gated: bfloat16 [4, 1024, 2048], P('dp', 'ctx')
- grad_query: bfloat16 [4, 1024, 2048], P('dp', 'ctx')
- grad_keys: bfloat16 [4, 1024, 2048], P('dp', 'ctx')
- grad_values: bfloat16 [4, 1024, 2048], P('dp', 'ctx')
- grad_filter: float32 [1024, 2048], P('ctx', 'dp')
- grad_short: float32 [3, 3, 2048], replicated
- grad_skip: float32 [2048], replicated
Inputs may be any that keep to these rules, and one draw needn't show every extreme that they name: Each row lists, in order, the lengths of the 16 documents packed into one sequence; they sum to 1024 and the longest is exactly 256. `long_filter`: one filter for every channel over the lags 0 .. 1023.
All inputs are finite; a program needn't handle non-finite values.
Results may differ from a plain program's by a relative error of at most 0.024.
Values may be sent and summed in bfloat16 or wider, within the bound.
No kernel may reach another device: no remote copies, remote signals or barrier semaphores. Data moves between devices by JAX's collectives and lax.ppermute only.
A program may use at most 192 MiB of HBM per device.

v0:
```python
import jax
import jax.numpy as jnp
from jax import lax
from jax.sharding import PartitionSpec as P


def shifted(x, axis, by):
    length = lax.axis_size(axis)
    pairs = [(i, i + by) for i in range(length) if 0 <= i + by < length]
    return lax.ppermute(x, axis, pairs)


def angles(time_idx, freq_idx, modulus, twist):
    turns = 2 * (time_idx * freq_idx % modulus) - twist * time_idx
    return jnp.pi * turns.astype(jnp.float32) / modulus


def table_halves(table):
    upper = lax.optimization_barrier(table.astype(jnp.bfloat16))
    lower = (table - upper.astype(jnp.float32)).astype(jnp.bfloat16)
    return (upper, lower)


def split_product(form, table, data):
    upper, lower = table_halves(table)
    if data.dtype == jnp.bfloat16:
        total = jnp.einsum(form, upper, data, preferred_element_type=jnp.float32)
        return total + jnp.einsum(form, lower, data, preferred_element_type=jnp.float32)
    data_upper = lax.optimization_barrier(data.astype(jnp.bfloat16))
    data_lower = (data - data_upper.astype(jnp.float32)).astype(jnp.bfloat16)
    total = jnp.einsum(form, upper, data_upper, preferred_element_type=jnp.float32)
    total = total + jnp.einsum(form, lower, data_upper, preferred_element_type=jnp.float32)
    return total + jnp.einsum(form, upper, data_lower, preferred_element_type=jnp.float32)


def dft_block(rows, direction):
    steps = jnp.arange(rows, dtype=jnp.int32)
    phase = angles(steps[:, None], steps[None, :], rows, 0)
    cosine = jnp.cos(phase)
    sine = direction * jnp.sin(phase)
    upper = jnp.concatenate([cosine, sine], 1)
    lower = jnp.concatenate([-sine, cosine], 1)
    return jnp.concatenate([upper, lower], 0)


def to_columns(data):
    return lax.all_to_all(data, "ctx", split_axis=0, concat_axis=0, tiled=True)


def to_rows(data):
    return lax.all_to_all(data, "ctx", split_axis=0, concat_axis=0, tiled=True)


def forward_spectrum(columns, index):
    parts, block, chans = columns.shape
    rows = parts * block
    seq_len = rows * parts
    time_p = jnp.arange(parts, dtype=jnp.int32)[None, :]
    freq_k = jnp.arange(parts, dtype=jnp.int32)[:, None]
    tables = []
    for twist in range(2):
        phase = angles(time_p, freq_k, parts, twist)
        tables.append(jnp.cos(phase))
        tables.append(-jnp.sin(phase))
    table = jnp.stack(tables).reshape(4 * parts, parts)
    flat = columns.reshape(parts, block * chans)
    partial_value = split_product("kp,pm->km", table, flat)
    partial_value = partial_value.reshape(2, 2, parts, block, chans)
    local_m = index * block + jnp.arange(block, dtype=jnp.int32)
    twiddled = []
    for twist in range(2):
        phase = angles(local_m[None, :], freq_k, seq_len, twist)[:, :, None]
        cosine = jnp.cos(phase)
        sine = jnp.sin(phase)
        real_part = partial_value[twist, 0]
        imag_part = partial_value[twist, 1]
        twiddled.append(real_part * cosine + imag_part * sine)
        twiddled.append(imag_part * cosine - real_part * sine)
    moved = lax.all_to_all(jnp.stack(twiddled), "ctx", split_axis=1, concat_axis=2, tiled=True)
    data = moved.reshape(2, 2 * rows, chans)
    spectrum = split_product("ab,sbc->sac", dft_block(rows, 1.0), data)
    return spectrum.reshape(2, 2, rows, chans)


def inverse_spectrum(spectrum, index, parts):
    rows, chans = (spectrum.shape[2], spectrum.shape[3])
    block = rows // parts
    seq_len = rows * parts
    data = spectrum.reshape(2, 2 * rows, chans)
    back = split_product("ab,sbc->sac", dft_block(rows, -1.0), data).reshape(2, 2, rows, chans)
    local_m = jnp.arange(rows, dtype=jnp.int32)[:, None]
    twisted = []
    for twist in range(2):
        phase = angles(local_m, index, seq_len, twist)
        cosine = jnp.cos(phase)
        sine = jnp.sin(phase)
        real_part = back[twist, 0]
        imag_part = back[twist, 1]
        twisted.append(real_part * cosine - imag_part * sine)
        twisted.append(imag_part * cosine + real_part * sine)
    stacked = jnp.stack(twisted).reshape(4, parts, block, chans)
    moved = (
        lax.all_to_all(stacked.astype(jnp.bfloat16), "ctx", split_axis=1, concat_axis=2, tiled=True)
        .astype(stacked.dtype)
        .reshape(4 * parts, block * chans)
    )
    time_p = jnp.arange(parts, dtype=jnp.int32)[:, None]
    freq_k = jnp.arange(parts, dtype=jnp.int32)[None, :]
    pieces = []
    for twist in range(2):
        phase = angles(time_p, freq_k, parts, twist)
        pieces.append(jnp.cos(phase))
        pieces.append(-jnp.sin(phase))
    table = jnp.stack(pieces, axis=1).reshape(parts, 4 * parts) / (2.0 * seq_len)
    result = split_product("kp,pm->km", table, moved)
    return result.reshape(parts, block, chans)


def spectrum_of(signal, index, parts):
    rows, channels = signal.shape
    columns = to_columns(signal).reshape(parts, rows // parts, channels)
    return forward_spectrum(columns, index)


def signal_of(spectrum, index, parts):
    rows, channels = (spectrum.shape[2], spectrum.shape[3])
    return to_rows(inverse_spectrum(spectrum, index, parts).reshape(rows, channels))


def complex_product(left_re, left_im, right_re, right_im, conjugate_left):
    if conjugate_left:
        return (left_re * right_re + left_im * right_im, left_re * right_im - left_im * right_re)
    return (left_re * right_re - left_im * right_im, left_re * right_im + left_im * right_re)


def spectral_product(first, second, conjugate_left):
    twists = []
    for twist in range(2):
        twists.append(
            jnp.stack(
                complex_product(
                    first[twist, 0],
                    first[twist, 1],
                    second[twist, 0],
                    second[twist, 1],
                    conjugate_left,
                )
            )
        )
    return jnp.stack(twists)


def short_forward(padded, weights, valid):
    count = weights.shape[0]
    rows = padded.shape[0] - count + 1
    wide = padded.astype(jnp.float32)
    summed = weights[0] * wide[count - 1 :]
    for offset in range(1, count):
        begin = count - 1 - offset
        summed = summed + jnp.where(
            valid[offset][:, None], weights[offset] * wide[begin : begin + rows], 0.0
        )
    return summed


def short_backward(padded, grad_short, after, weights, valid, valid_after):
    count = weights.shape[0]
    rows = grad_short.shape[0]
    wide = padded.astype(jnp.float32)
    extended = jnp.concatenate([grad_short, after], 0)
    grad_source = weights[0] * grad_short
    weight_grads = [jnp.sum(wide[count - 1 :] * grad_short, axis=0)]
    for offset in range(1, count):
        later = jnp.where(
            valid_after[offset, offset : offset + rows][:, None],
            extended[offset : offset + rows],
            0.0,
        )
        grad_source = grad_source + weights[offset] * later
        masked = jnp.where(valid[offset][:, None], grad_short, 0.0)
        begin = count - 1 - offset
        weight_grads.append(jnp.sum(masked * wide[begin : begin + rows], axis=0))
    return (grad_source, jnp.stack(weight_grads))


def local(query, keys, values, cotangent, long_filter, short_weights, skip, lengths):
    parts = lax.axis_size("ctx")
    index = lax.axis_index("ctx")
    groups = lax.axis_size("dp")
    q_rows = query[0]
    k_rows = keys[0]
    v_rows = values[0]
    upstream = cotangent[0].astype(jnp.float32)
    rows, chans = q_rows.shape
    taps = short_weights.shape[1]
    seq_len = rows * parts
    doc_len = lengths[0]
    starts = jnp.cumsum(doc_len) - doc_len

    def valid_mask(where):
        begin = jnp.max(jnp.where(starts[None, :] <= where[:, None], starts[None, :], 0), axis=1)
        shifts = jnp.arange(taps, dtype=jnp.int32)[:, None]
        return where[None, :] - shifts >= begin[None, :]

    position = index * rows + jnp.arange(rows, dtype=jnp.int32)
    valid = valid_mask(position)
    valid_after = valid_mask(index * rows + jnp.arange(rows + taps - 1, dtype=jnp.int32))
    edge = rows - taps + 1
    rim = shifted((q_rows[edge:], k_rows[edge:], v_rows[edge:]), "ctx", 1)
    padded_q = jnp.concatenate([rim[0], q_rows], 0)
    padded_k = jnp.concatenate([rim[1], k_rows], 0)
    padded_v = jnp.concatenate([rim[2], v_rows], 0)
    q_short = (
        short_forward(padded_q, short_weights[0], valid).astype(jnp.bfloat16).astype(jnp.float32)
    )
    k_short = (
        short_forward(padded_k, short_weights[1], valid).astype(jnp.bfloat16).astype(jnp.float32)
    )
    v_short = (
        short_forward(padded_v, short_weights[2], valid).astype(jnp.bfloat16).astype(jnp.float32)
    )
    mixed = (k_short * v_short).astype(jnp.bfloat16)
    grad_conv = (upstream * q_short).astype(jnp.bfloat16)
    mixed_wide = mixed.astype(jnp.float32)
    grad_wide = grad_conv.astype(jnp.float32)
    spectrum_f = spectrum_of(long_filter, index, parts)
    spectrum_x = spectrum_of(mixed, index, parts)
    spectrum_g = spectrum_of(grad_conv, index, parts)
    conv_spec = spectral_product(spectrum_x, spectrum_f, False)
    back_spec = spectral_product(spectrum_f, spectrum_g, True)
    cross_spec = spectral_product(spectrum_x, spectrum_g, True)
    conv_raw = signal_of(conv_spec, index, parts)
    back_raw = signal_of(back_spec, index, parts)
    lagged = signal_of(cross_spec, index, parts)
    filter_part = lax.psum_scatter(
        lagged.astype(jnp.bfloat16), "dp", scatter_dimension=1, tiled=True
    ).astype(jnp.float32)
    conv = conv_raw + skip * mixed_wide
    gated = (q_short * conv).astype(jnp.bfloat16)
    grad_qs = upstream * conv
    grad_mixed = back_raw + skip * grad_wide
    grad_ks = grad_mixed * v_short
    grad_vs = grad_mixed * k_short
    skip_grad = jnp.sum(grad_wide * mixed_wide, axis=0)
    head = taps - 1
    after = shifted((grad_qs[:head], grad_ks[:head], grad_vs[:head]), "ctx", -1)
    grad_q, short_q = short_backward(
        padded_q, grad_qs, after[0], short_weights[0], valid, valid_after
    )
    grad_k, short_k = short_backward(
        padded_k, grad_ks, after[1], short_weights[1], valid, valid_after
    )
    grad_v, short_v = short_backward(
        padded_v, grad_vs, after[2], short_weights[2], valid, valid_after
    )
    summed = lax.psum((jnp.stack([short_q, short_k, short_v]), skip_grad), ("dp", "ctx"))
    scale = 1.0 / (groups * seq_len)
    return (
        gated[None],
        grad_q.astype(jnp.bfloat16)[None],
        grad_k.astype(jnp.bfloat16)[None],
        grad_v.astype(jnp.bfloat16)[None],
        filter_part * scale,
        summed[0] * scale,
        summed[1] * scale,
    )


def solution(mesh):
    in_specs = (
        P("dp", "ctx", None),
        P("dp", "ctx", None),
        P("dp", "ctx", None),
        P("dp", "ctx", None),
        P("ctx", None),
        P(),
        P(),
        P("dp", None),
    )
    out_specs = (
        P("dp", "ctx", None),
        P("dp", "ctx", None),
        P("dp", "ctx", None),
        P("dp", "ctx", None),
        P("ctx", "dp"),
        P(),
        P(),
    )
    return jax.shard_map(local, mesh=mesh, in_specs=in_specs, out_specs=out_specs, check_vma=False)
```

profile of v0, /device:TPU:8, one launch (start us, length us, event | category | flops | bytes accessed | tf_op | source)
XLA Modules:
  0.0 839.3 jit_solution(11256855569213254024)
XLA Ops:
  37.6 4.9 all-to-all-start
  45.8 9.1 %all-to-all-done = bf16[8,16,2048]{2,1,0:T(8,128)(2,1)S(1)} async-done(((bf16[8,16,2048]{2,1,0:T(8,128)(2,1)}), bf16[8,16,2048]{2,1,0:T(8,128)(2,1)S(1)}, u32[]{:S(2)}, u32[]{:S(2)}) %all-to-all-start) | async-done | bytes 524320 | tf_op jit(solution)/shard_map/all_to_all | solution.py:47
  55.0 5.1 all-to-all-start.6
  63.8 8.6 %all-to-all-done.6 = bf16[8,16,2048]{2,1,0:T(8,128)(2,1)S(1)} async-done(((bf16[8,16,2048]{2,1,0:T(8,128)(2,1)}), bf16[8,16,2048]{2,1,0:T(8,128)(2,1)S(1)}, u32[]{:S(2)}, u32[]{:S(2)}) %all-to-all-start.6) | async-done | bytes 524320 | tf_op jit(solution)/shard_map/all_to_all | solution.py:47
  76.2 5.5 multiply_add_fusion.1
  81.8 6.2 multiply_add_fusion
  90.3 5.9 all-to-all-start.3
  100.2 85.5 %all-to-all-done.3 = f32[4,8,16,2048]{3,2,0,1:T(8,128)} async-done(((f32[4,8,16,2048]{3,2,0,1:T(8,128)}), f32[4,8,16,2048]{3,2,0,1:T(8,128)}, u32[]{:S(2)}, u32[]{:S(2)}) %all-to-all-start.3) | async-done | bytes 4194336 | tf_op jit(solution)/shard_map/all_to_all | solution.py:79
  185.7 7.0 all-to-all-start.1
  196.2 86.5 %all-to-all-done.1 = f32[4,8,16,2048]{3,2,0,1:T(8,128)} async-done(((f32[4,8,16,2048]{3,2,0,1:T(8,128)}), f32[4,8,16,2048]{3,2,0,1:T(8,128)}, u32[]{:S(2)}, u32[]{:S(2)}) %all-to-all-start.1) | async-done | bytes 4194336 | tf_op jit(solution)/shard_map/all_to_all | solution.py:79
  282.7 7.0 all-to-all-start.7
  311.9 67.9 %all-to-all-done.7 = f32[4,8,16,2048]{3,2,0,1:T(8,128)} async-done(((f32[4,8,16,2048]{3,2,0,1:T(8,128)}), f32[4,8,16,2048]{3,2,0,1:T(8,128)}, u32[]{:S(2)}, u32[]{:S(2)}) %all-to-all-start.7) | async-done | bytes 4194336 | tf_op jit(solution)/shard_map/all_to_all | solution.py:79
  442.9 6.6 all-to-all-start.4
  452.3 43.1 %all-to-all-done.4 = bf16[4,8,16,2048]{3,2,0,1:T(8,128)(2,1)S(1)} async-done(((bf16[4,8,16,2048]{3,2,0,1:T(8,128)(2,1)}), bf16[4,8,16,2048]{3,2,0,1:T(8,128)(2,1)S(1)}, u32[]{:S(2)}, u32[]{:S(2)}) %all-to-all-start.4) | async-done | bytes 2097184 | tf_op jit(solution)/shard_map/all_to_all | solution.py:103
  496.8 6.1 all-to-all-start.8
  505.7 43.2 %all-to-all-done.8 = bf16[4,8,16,2048]{3,2,0,1:T(8,128)(2,1)S(1)} async-done(((bf16[4,8,16,2048]{3,2,0,1:T(8,128)(2,1)}), bf16[4,8,16,2048]{3,2,0,1:T(8,128)(2,1)S(1)}, u32[]{:S(2)}, u32[]{:S(2)}) %all-to-all-start.8) | async-done | bytes 2097184 | tf_op jit(solution)/shard_map/all_to_all | solution.py:103
  550.2 6.1 all-to-all-start.10
  562.3 39.9 %all-to-all-done.10 = bf16[4,8,16,2048]{3,2,0,1:T(8,128)(2,1)S(1)} async-done(((bf16[4,8,16,2048]{3,2,0,1:T(8,128)(2,1)}), bf16[4,8,16,2048]{3,2,0,1:T(8,128)(2,1)S(1)}, u32[]{:S(2)}, u32[]{:S(2)}) %all-to-all-start.10) | async-done | bytes 2097184 | tf_op jit(solution)/shard_map/all_to_all | solution.py:103
  602.2 6.1 all-to-all-start.5
  614.2 17.7 %all-to-all-done.5 = f32[8,16,2048]{2,1,0:T(8,128)S(1)} async-done(((f32[8,16,2048]{2,1,0:T(8,128)}), f32[8,16,2048]{2,1,0:T(8,128)S(1)}, u32[]{:S(2)}, u32[]{:S(2)}) %all-to-all-start.5) | async-done | bytes 1048608 | tf_op jit(solution)/shard_map/all_to_all | solution.py:51
  632.9 6.0 all-to-all-start.9
  639.1 43.9 %psum.15 = f32[2048]{0:T(1024)S(1)} all-reduce(f32[2048]{0:T(1024)S(1)} %copy-done.61), channel_id=1, replica_groups=mesh['dp'=4,'ctx'=8] {'dp','ctx'}, use_global_device_ids=true, to_apply=%region_15.16 | all-reduce | flops 2048 | bytes 16384 | tf_op jit(solution)/shard_map/psum | solution.py:256
  690.3 7.4 all-to-all-start.11
  722.6 105.8 %all-reduce.2.cloned.1.call-done = f32[3,3,2048]{2,1,0:T(4,128)} async-done(((f32[3,3,2048]{2,1,0:T(4,128)}), f32[3,3,2048]{2,1,0:T(4,128)}) %all-reduce.2.cloned.1.call-update) | async-done | bytes 73744 | tf_op jit(solution)/shard_map/psum | solution.py:256
  (288 shorter events, 191.2 us)
Async XLA Ops:
  8.8 19.9 %collective-permute-start = (bf16[2,2048]{1,0:T(2,128)(2,1)S(1)}, bf16[2,2048]{1,0:T(2,128)(2,1)S(1)}, u32[]{:S(2)}, u32[]{:S(2)}) collective-permute-start(bf16[2,2048]{1,0:T(2,128)(2,1)S(1)} %slice_bitcast_fusion.2), channel_id=1, source_target_pairs={{0,1},{1,2},{2,3},{3,4},{4,5},{5,6},{6,7},{8,9},{9,10},{10,11},{11... | collective-permute-start | bytes 24584 | tf_op jit(solution)/shard_map/ppermute | solution.py:10
  13.1 16.9 %collective-permute-start.1 = (bf16[2,2048]{1,0:T(2,128)(2,1)S(1)}, bf16[2,2048]{1,0:T(2,128)(2,1)S(1)}, u32[]{:S(2)}, u32[]{:S(2)}) collective-permute-start(bf16[2,2048]{1,0:T(2,128)(2,1)S(1)} %slice_bitcast_fusion.1), channel_id=1, source_target_pairs={{0,1},{1,2},{2,3},{3,4},{4,5},{5,6},{6,7},{8,9},{9,10},{10,11},{11... | collective-permute-start | bytes 24584 | tf_op jit(solution)/shard_map/ppermute | solution.py:10
  17.3 12.9 %collective-permute-start.2 = (bf16[2,2048]{1,0:T(2,128)(2,1)S(1)}, bf16[2,2048]{1,0:T(2,128)(2,1)S(1)}, u32[]{:S(2)}, u32[]{:S(2)}) collective-permute-start(bf16[2,2048]{1,0:T(2,128)(2,1)S(1)} %slice_bitcast_fusion), channel_id=1, source_target_pairs={{0,1},{1,2},{2,3},{3,4},{4,5},{5,6},{6,7},{8,9},{9,10},{10,11},{11... | collective-permute-start | bytes 24584 | tf_op jit(solution)/shard_map/ppermute | solution.py:10
  20.7 16.8 %all-to-all-start.2 = ((bf16[8,16,2048]{2,1,0:T(8,128)(2,1)}), bf16[8,16,2048]{2,1,0:T(8,128)(2,1)S(1)}, u32[]{:S(2)}, u32[]{:S(2)}) async-start(bf16[8,16,2048]{2,1,0:T(8,128)(2,1)} %bitcast.384), calls=%async_computation.2 | async-start | bytes 1048576 | tf_op jit(solution)/shard_map/all_to_all | solution.py:47
  37.6 17.4 %all-to-all-start = ((bf16[8,16,2048]{2,1,0:T(8,128)(2,1)}), bf16[8,16,2048]{2,1,0:T(8,128)(2,1)S(1)}, u32[]{:S(2)}, u32[]{:S(2)}) async-start(bf16[8,16,2048]{2,1,0:T(8,128)(2,1)} %bitcast.19), calls=%async_computation | async-start | bytes 1048576 | tf_op jit(solution)/shard_map/all_to_all | solution.py:47
  55.0 17.4 %all-to-all-start.6 = ((bf16[8,16,2048]{2,1,0:T(8,128)(2,1)}), bf16[8,16,2048]{2,1,0:T(8,128)(2,1)S(1)}, u32[]{:S(2)}, u32[]{:S(2)}) async-start(bf16[8,16,2048]{2,1,0:T(8,128)(2,1)} %bitcast.64), calls=%async_computation.6 | async-start | bytes 1048576 | tf_op jit(solution)/shard_map/all_to_all | solution.py:47
  90.3 95.4 %all-to-all-start.3 = ((f32[4,8,16,2048]{3,2,0,1:T(8,128)}), f32[4,8,16,2048]{3,2,0,1:T(8,128)}, u32[]{:S(2)}, u32[]{:S(2)}) async-start(f32[4,8,16,2048]{3,2,0,1:T(8,128)} %pad_maximum_fusion.1), calls=%async_computation.3 | async-start | bytes 8388608 | tf_op jit(solution)/shard_map/all_to_all | solution.py:79
  100.2 92.5 %copy-start.23 = (f32[1,8,16,2048]{3,2,0,1:T(8,128)S(1)}, f32[1,8,16,2048]{3,2,0,1:T(8,128)}, u32[]{:S(2)}) copy-start(f32[1,8,16,2048]{3,2,0,1:T(8,128)} %get-tuple-element.70) | copy-start | bytes 3145732
  100.2 92.5 %copy-start.31 = (f32[1,8,16,2048]{3,2,0,1:T(8,128)S(1)}, f32[1,8,16,2048]{3,2,0,1:T(8,128)}, u32[]{:S(2)}) copy-start(f32[1,8,16,2048]{3,2,0,1:T(8,128)} %get-tuple-element.71) | copy-start | bytes 3145732
  185.7 97.1 %all-to-all-start.1 = ((f32[4,8,16,2048]{3,2,0,1:T(8,128)}), f32[4,8,16,2048]{3,2,0,1:T(8,128)}, u32[]{:S(2)}, u32[]{:S(2)}) async-start(f32[4,8,16,2048]{3,2,0,1:T(8,128)} %pad_maximum_fusion), calls=%async_computation.1 | async-start | bytes 8388608 | tf_op jit(solution)/shard_map/all_to_all | solution.py:79
  282.7 97.1 %all-to-all-start.7 = ((f32[4,8,16,2048]{3,2,0,1:T(8,128)}), f32[4,8,16,2048]{3,2,0,1:T(8,128)}, u32[]{:S(2)}, u32[]{:S(2)}) async-start(f32[4,8,16,2048]{3,2,0,1:T(8,128)} %pad_maximum_fusion.3), calls=%async_computation.7 | async-start | bytes 8388608 | tf_op jit(solution)/shard_map/all_to_all | solution.py:79
  442.9 52.5 %all-to-all-start.4 = ((bf16[4,8,16,2048]{3,2,0,1:T(8,128)(2,1)}), bf16[4,8,16,2048]{3,2,0,1:T(8,128)(2,1)S(1)}, u32[]{:S(2)}, u32[]{:S(2)}) async-start(bf16[4,8,16,2048]{3,2,0,1:T(8,128)(2,1)} %pad_maximum_fusion.8), calls=%async_computation.4 | async-start | bytes 4194304 | tf_op jit(solution)/shard_map/all_to_all | solution.py:103
  452.3 50.6 %copy-start.37 = (bf16[1,8,16,2048]{3,2,0,1:T(8,128)(2,1)S(1)}, bf16[1,8,16,2048]{3,2,0,1:T(8,128)(2,1)}, u32[]{:S(2)}) copy-start(bf16[1,8,16,2048]{3,2,0,1:T(8,128)(2,1)} %get-tuple-element.61) | copy-start | bytes 1572868
  452.3 50.6 %copy-start.38 = (bf16[1,8,16,2048]{3,2,0,1:T(8,128)(2,1)S(1)}, bf16[1,8,16,2048]{3,2,0,1:T(8,128)(2,1)}, u32[]{:S(2)}) copy-start(bf16[1,8,16,2048]{3,2,0,1:T(8,128)(2,1)} %get-tuple-element.62) | copy-start | bytes 1572868
  496.8 52.1 %all-to-all-start.8 = ((bf16[4,8,16,2048]{3,2,0,1:T(8,128)(2,1)}), bf16[4,8,16,2048]{3,2,0,1:T(8,128)(2,1)S(1)}, u32[]{:S(2)}, u32[]{:S(2)}) async-start(bf16[4,8,16,2048]{3,2,0,1:T(8,128)(2,1)} %pad_maximum_fusion.11), calls=%async_computation.8 | async-start | bytes 4194304 | tf_op jit(solution)/shard_map/all_to_all | solution.py:103
  550.2 52.1 %all-to-all-start.10 = ((bf16[4,8,16,2048]{3,2,0,1:T(8,128)(2,1)}), bf16[4,8,16,2048]{3,2,0,1:T(8,128)(2,1)S(1)}, u32[]{:S(2)}, u32[]{:S(2)}) async-start(bf16[4,8,16,2048]{3,2,0,1:T(8,128)(2,1)} %pad_maximum_fusion.14), calls=%async_computation.10 | async-start | bytes 4194304 | tf_op jit(solution)/shard_map/all_to_all | solution.py:103
  602.2 29.7 %all-to-all-start.5 = ((f32[8,16,2048]{2,1,0:T(8,128)}), f32[8,16,2048]{2,1,0:T(8,128)S(1)}, u32[]{:S(2)}, u32[]{:S(2)}) async-start(f32[8,16,2048]{2,1,0:T(8,128)} %copy.115), calls=%async_computation.5 | async-start | bytes 2097152 | tf_op jit(solution)/shard_map/all_to_all | solution.py:51
  632.9 57.4 %all-to-all-start.9 = ((f32[8,16,2048]{2,1,0:T(8,128)}), f32[8,16,2048]{2,1,0:T(8,128)S(1)}, u32[]{:S(2)}, u32[]{:S(2)}) async-start(f32[8,16,2048]{2,1,0:T(8,128)} %copy.122), calls=%async_computation.9 | async-start | bytes 2097152 | tf_op jit(solution)/shard_map/all_to_all | solution.py:51
  690.3 19.1 %all-to-all-start.11 = ((bf16[8,16,2048]{2,1,0:T(8,128)(2,1)}), bf16[8,16,2048]{2,1,0:T(8,128)(2,1)}, u32[]{:S(2)}, u32[]{:S(2)}) async-start(bf16[8,16,2048]{2,1,0:T(8,128)(2,1)} %copy.124), calls=%async_computation.11 | async-start | bytes 1048576 | tf_op jit(solution)/shard_map/all_to_all | solution.py:51
  697.7 130.7 %all-reduce.2.cloned.1.call-start = ((), (), s32[]{:S(2)}) async-start(), calls=%async_computation.14 | async-start | bytes 196608 | tf_op jit(solution)/shard_map/psum | solution.py:256
  702.4 127.5 %reduce-scatter.2.cloned.1.call-start = ((), (), s32[]{:S(2)}) async-start(), calls=%async_computation.13 | async-start | bytes 655360 | tf_op jit(solution)/shard_map/reduce_scatter | solution.py:235
  703.3 13.7 %collective-permute-start.3 = (f32[2,2048]{1,0:T(2,128)S(1)}, f32[2,2048]{1,0:T(2,128)S(1)}, u32[]{:S(2)}, u32[]{:S(2)}) collective-permute-start(f32[2,2048]{1,0:T(2,128)S(1)} %slice.390), channel_id=1, source_target_pairs={{1,0},{2,1},{3,2},{4,3},{5,4},{6,5},{7,6},{9,8},{10,9},{11,10},{12... | collective-permute-start | bytes 49160 | tf_op jit(solution)/shard_map/ppermute | solution.py:10
  710.3 10.1 %collective-permute-start.4 = (f32[2,2048]{1,0:T(2,128)S(1)}, f32[2,2048]{1,0:T(2,128)S(1)}, u32[]{:S(2)}, u32[]{:S(2)}) collective-permute-start(f32[2,2048]{1,0:T(2,128)S(1)} %slice.406), channel_id=1, source_target_pairs={{1,0},{2,1},{3,2},{4,3},{5,4},{6,5},{7,6},{9,8},{10,9},{11,10},{12... | collective-permute-start | bytes 49160 | tf_op jit(solution)/shard_map/ppermute | solution.py:10
  714.3 6.1 collective-permute-start.5
  (65 other events, 434.9 us)
Sparse Core Ops, SparseCore 0:
  705.6 122.7 all-reduce.1
Sparse Core Ops, SparseCore 1:
  709.6 21.2 reduce-scatter.1
where the time goes:
time: 846 us; the launch traced here: 839 us
  waiting for transfers between devices  512 us (61%)
  starting transfers between devices  93 us (11%)
  other arithmetic  65.8 us (8%)
  matrix products  55.6 us (7%)
  local copies, waits for them, and re-layouts  52.2 us (6%)
  blocking collectives  43.9 us (5%)
  between operations  16.9 us (2%)
    all_to_all x3, waiting for transfers between devices, forward_spectrum(): lax.all_to_all(jnp.stack(twiddled), 'ctx', split_axis=1, concat_axis=2, t...  240 us
    all_to_all x3, waiting for transfers between devices, inverse_spectrum(): lax.all_to_all(stacked.astype(jnp.bfloat16), 'ctx', split_axis=1, concat_...  126 us
    psum x1, waiting for transfers between devices, local(): lax.psum((jnp.stack([short_q, short_k, short_v]), skip_grad), ('dp', 'ctx'))  106 us
    psum x1, blocking collectives, local(): lax.psum((jnp.stack([short_q, short_k, short_v]), skip_grad), ('dp', 'ctx'))  43.9 us
    unnamed x144, local copies, waits for them, and re-layouts  22.3 us
    ppermute x6, starting transfers between devices, shifted(): return lax.ppermute(x, axis, pairs)  20.3 us
    dot_general x9, matrix products, split_product(): jnp.einsum(form, upper, data_lower, preferred_element_type=jnp.float32)  20 us
    all_to_all x3, waiting for transfers between devices, to_columns(): return lax.all_to_all(data, 'ctx', split_axis=0, concat_axis=0, tiled=True)  20 us
  transfers between devices with their start and end apart: 20, of which 12 were waited for; matrix products, arithmetic and copies ran while one was open for 10% of the time, Pallas kernels for 0%

commit v1 on v0

--- a/solution.py
+++ b/solution.py
@@ -253,7 +253,7 @@
     grad_v, short_v = short_backward(
         padded_v, grad_vs, after[2], short_weights[2], valid, valid_after
     )
-    summed = lax.psum((jnp.stack([short_q, short_k, short_v]), skip_grad), ("dp", "ctx"))
+    summed = lax.psum(lax.psum((jnp.stack([short_q, short_k, short_v]), skip_grad), "ctx"), "dp")
     scale = 1.0 / (groups * seq_len)
     return (
         gated[None],

time: 846 us -> 817 us (0.966)
  blocking collectives: 43.9 us -> 24.7 us
    psum x1 -> x2, waiting for transfers between devices: 106 us -> 61.1 us  [the longest x1 41.5 us: local(): lax.psum((jnp.stack([short_q, short_k, short_v]), skip_grad), 'ctx')]
    reduce_scatter x1, waiting for transfers between devices: 0.01 us -> 22.7 us  [local(): lax.psum_scatter(lagged.astype(jnp.bfloat16), 'dp', scatter_dimension=1,...]
    psum x1 -> x2, blocking collectives: 43.9 us -> 24.7 us  [the longest x1 18.9 us: local(): lax.psum((jnp.stack([short_q, short_k, short_v]), skip_grad), 'ctx')]
    all_to_all x3, waiting for transfers between devices: 19.9 us -> 34 us  [to_rows(): return lax.all_to_all(data, 'ctx', split_axis=0, concat_axis=0, tiled=True)]
  transfers between devices with their start and end apart: 20 -> 21, of which waited for: 12 -> 14; matrix products, arithmetic and copies ran while one was open for 10% -> 10% of each run, Pallas kernels for 0% -> 0%
where the time goes in v1:
time: 817 us; the launch traced here: 809 us
  waiting for transfers between devices  504 us (62%)
  starting transfers between devices  91.4 us (11%)
  other arithmetic  65.9 us (8%)
  matrix products  55.5 us (7%)
  local copies, waits for them, and re-layouts  52 us (6%)
  blocking collectives  24.7 us (3%)
  between operations  15.2 us (2%)
    all_to_all x3, waiting for transfers between devices, forward_spectrum(): lax.all_to_all(jnp.stack(twiddled), 'ctx', split_axis=1, concat_axis=2, t...  240 us
    all_to_all x3, waiting for transfers between devices, inverse_spectrum(): lax.all_to_all(stacked.astype(jnp.bfloat16), 'ctx', split_axis=1, concat_...  126 us
    psum x1, waiting for transfers between devices, local(): lax.psum((jnp.stack([short_q, short_k, short_v]), skip_grad), 'ctx')  41.5 us
    all_to_all x3, waiting for transfers between devices, to_rows(): return lax.all_to_all(data, 'ctx', split_axis=0, concat_axis=0, tiled=True)  34 us
    reduce_scatter x1, waiting for transfers between devices, local(): lax.psum_scatter(lagged.astype(jnp.bfloat16), 'dp', scatter_dimension=1,...  22.7 us
    unnamed x144, local copies, waits for them, and re-layouts  22.2 us
    all_to_all x3, waiting for transfers between devices, to_columns(): return lax.all_to_all(data, 'ctx', split_axis=0, concat_axis=0, tiled=True)  20.1 us
    dot_general x9, matrix products, split_product(): jnp.einsum(form, upper, data_lower, preferred_element_type=jnp.float32)  20 us
  transfers between devices with their start and end apart: 21, of which 14 were waited for; matrix products, arithmetic and copies ran while one was open for 10% of the time, Pallas kernels for 0%

profile of v1, /device:TPU:8, one launch (start us, length us, event | category | flops | bytes accessed | tf_op | source)
XLA Modules:
  0.0 808.9 jit_solution(11520513715500787769)
XLA Ops:
  45.0 9.1 %all-to-all-done = bf16[8,16,2048]{2,1,0:T(8,128)(2,1)S(1)} async-done(((bf16[8,16,2048]{2,1,0:T(8,128)(2,1)}), bf16[8,16,2048]{2,1,0:T(8,128)(2,1)S(1)}, u32[]{:S(2)}, u32[]{:S(2)}) %all-to-all-start) | async-done | bytes 524320 | tf_op jit(solution)/shard_map/all_to_all | solution.py:47
  63.0 8.6 %all-to-all-done.6 = bf16[8,16,2048]{2,1,0:T(8,128)(2,1)S(1)} async-done(((bf16[8,16,2048]{2,1,0:T(8,128)(2,1)}), bf16[8,16,2048]{2,1,0:T(8,128)(2,1)S(1)}, u32[]{:S(2)}, u32[]{:S(2)}) %all-to-all-start.6) | async-done | bytes 524320 | tf_op jit(solution)/shard_map/all_to_all | solution.py:47
  80.9 6.2 multiply_add_fusion
  89.5 5.9 all-to-all-start.3
  99.4 85.5 %all-to-all-done.3 = f32[4,8,16,2048]{3,2,0,1:T(8,128)} async-done(((f32[4,8,16,2048]{3,2,0,1:T(8,128)}), f32[4,8,16,2048]{3,2,0,1:T(8,128)}, u32[]{:S(2)}, u32[]{:S(2)}) %all-to-all-start.3) | async-done | bytes 4194336 | tf_op jit(solution)/shard_map/all_to_all | solution.py:79
  184.9 7.0 all-to-all-start.1
  195.4 86.5 %all-to-all-done.1 = f32[4,8,16,2048]{3,2,0,1:T(8,128)} async-done(((f32[4,8,16,2048]{3,2,0,1:T(8,128)}), f32[4,8,16,2048]{3,2,0,1:T(8,128)}, u32[]{:S(2)}, u32[]{:S(2)}) %all-to-all-start.1) | async-done | bytes 4194336 | tf_op jit(solution)/shard_map/all_to_all | solution.py:79
  281.9 7.0 all-to-all-start.7
  311.1 68.0 %all-to-all-done.7 = f32[4,8,16,2048]{3,2,0,1:T(8,128)} async-done(((f32[4,8,16,2048]{3,2,0,1:T(8,128)}), f32[4,8,16,2048]{3,2,0,1:T(8,128)}, u32[]{:S(2)}, u32[]{:S(2)}) %all-to-all-start.7) | async-done | bytes 4194336 | tf_op jit(solution)/shard_map/all_to_all | solution.py:79
  442.1 6.6 all-to-all-start.4
  451.5 43.1 %all-to-all-done.4 = bf16[4,8,16,2048]{3,2,0,1:T(8,128)(2,1)S(1)} async-done(((bf16[4,8,16,2048]{3,2,0,1:T(8,128)(2,1)}), bf16[4,8,16,2048]{3,2,0,1:T(8,128)(2,1)S(1)}, u32[]{:S(2)}, u32[]{:S(2)}) %all-to-all-start.4) | async-done | bytes 2097184 | tf_op jit(solution)/shard_map/all_to_all | solution.py:103
  496.0 6.1 all-to-all-start.8
  504.9 43.1 %all-to-all-done.8 = bf16[4,8,16,2048]{3,2,0,1:T(8,128)(2,1)S(1)} async-done(((bf16[4,8,16,2048]{3,2,0,1:T(8,128)(2,1)}), bf16[4,8,16,2048]{3,2,0,1:T(8,128)(2,1)S(1)}, u32[]{:S(2)}, u32[]{:S(2)}) %all-to-all-start.8) | async-done | bytes 2097184 | tf_op jit(solution)/shard_map/all_to_all | solution.py:103
  549.4 6.1 all-to-all-start.10
  561.5 39.9 %all-to-all-done.10 = bf16[4,8,16,2048]{3,2,0,1:T(8,128)(2,1)S(1)} async-done(((bf16[4,8,16,2048]{3,2,0,1:T(8,128)(2,1)}), bf16[4,8,16,2048]{3,2,0,1:T(8,128)(2,1)S(1)}, u32[]{:S(2)}, u32[]{:S(2)}) %all-to-all-start.10) | async-done | bytes 2097184 | tf_op jit(solution)/shard_map/all_to_all | solution.py:103
  601.4 6.1 all-to-all-start.5
  613.3 17.8 %all-to-all-done.5 = f32[8,16,2048]{2,1,0:T(8,128)S(1)} async-done(((f32[8,16,2048]{2,1,0:T(8,128)}), f32[8,16,2048]{2,1,0:T(8,128)S(1)}, u32[]{:S(2)}, u32[]{:S(2)}) %all-to-all-start.5) | async-done | bytes 1048608 | tf_op jit(solution)/shard_map/all_to_all | solution.py:51
  632.1 6.0 all-to-all-start.9
  645.4 16.2 %all-to-all-done.9 = f32[8,16,2048]{2,1,0:T(8,128)S(1)} async-done(((f32[8,16,2048]{2,1,0:T(8,128)}), f32[8,16,2048]{2,1,0:T(8,128)S(1)}, u32[]{:S(2)}, u32[]{:S(2)}) %all-to-all-start.9) | async-done | bytes 1048608 | tf_op jit(solution)/shard_map/all_to_all | solution.py:51
  661.6 6.4 all-to-all-start.11
  673.2 18.9 %psum.30 = f32[2048]{0:T(1024)S(1)} all-reduce(f32[2048]{0:T(1024)S(1)} %copy-done.61), channel_id=1, replica_groups=mesh['dp'=4,'ctx'=8] {'ctx'}, use_global_device_ids=true, to_apply=%region_16.17 | all-reduce | flops 2048 | bytes 16384 | tf_op jit(solution)/shard_map/psum | solution.py:256
  701.3 41.5 %all-reduce.3.cloned.1.call-done = f32[3,3,2048]{2,1,0:T(4,128)} async-done(((f32[3,3,2048]{2,1,0:T(4,128)}), f32[3,3,2048]{2,1,0:T(4,128)}) %all-reduce.3.cloned.1.call-update) | async-done | bytes 73744 | tf_op jit(solution)/shard_map/psum | solution.py:256
  756.5 19.7 %all-reduce.5.cloned.1.call-done = f32[3,3,2048]{2,1,0:T(4,128)} async-done(((f32[3,3,2048]{2,1,0:T(4,128)}), f32[3,3,2048]{2,1,0:T(4,128)}) %all-reduce.5.cloned.1.call-update) | async-done | bytes 73744 | tf_op jit(solution)/shard_map/psum | solution.py:256
  777.7 22.7 %reduce-scatter.2.cloned.1.call-done = bf16[128,512]{1,0:T(8,128)(2,1)} async-done(((bf16[128,2048]{1,0:T(8,128)(2,1)}), bf16[128,512]{1,0:T(8,128)(2,1)}) %reduce-scatter.2.cloned.1.call-update) | async-done | bytes 131088 | tf_op jit(solution)/shard_map/reduce_scatter | solution.py:235
  (292 shorter events, 209.6 us)
Async XLA Ops:
  8.0 19.8 %collective-permute-start = (bf16[2,2048]{1,0:T(2,128)(2,1)S(1)}, bf16[2,2048]{1,0:T(2,128)(2,1)S(1)}, u32[]{:S(2)}, u32[]{:S(2)}) collective-permute-start(bf16[2,2048]{1,0:T(2,128)(2,1)S(1)} %slice_bitcast_fusion.2), channel_id=1, source_target_pairs={{0,1},{1,2},{2,3},{3,4},{4,5},{5,6},{6,7},{8,9},{9,10},{10,11},{11... | collective-permute-start | bytes 24584 | tf_op jit(solution)/shard_map/ppermute | solution.py:10
  12.2 16.9 %collective-permute-start.1 = (bf16[2,2048]{1,0:T(2,128)(2,1)S(1)}, bf16[2,2048]{1,0:T(2,128)(2,1)S(1)}, u32[]{:S(2)}, u32[]{:S(2)}) collective-permute-start(bf16[2,2048]{1,0:T(2,128)(2,1)S(1)} %slice_bitcast_fusion.1), channel_id=1, source_target_pairs={{0,1},{1,2},{2,3},{3,4},{4,5},{5,6},{6,7},{8,9},{9,10},{10,11},{11... | collective-permute-start | bytes 24584 | tf_op jit(solution)/shard_map/ppermute | solution.py:10
  16.4 12.8 %collective-permute-start.2 = (bf16[2,2048]{1,0:T(2,128)(2,1)S(1)}, bf16[2,2048]{1,0:T(2,128)(2,1)S(1)}, u32[]{:S(2)}, u32[]{:S(2)}) collective-permute-start(bf16[2,2048]{1,0:T(2,128)(2,1)S(1)} %slice_bitcast_fusion), channel_id=1, source_target_pairs={{0,1},{1,2},{2,3},{3,4},{4,5},{5,6},{6,7},{8,9},{9,10},{10,11},{11... | collective-permute-start | bytes 24584 | tf_op jit(solution)/shard_map/ppermute | solution.py:10
  19.9 16.8 %all-to-all-start.2 = ((bf16[8,16,2048]{2,1,0:T(8,128)(2,1)}), bf16[8,16,2048]{2,1,0:T(8,128)(2,1)S(1)}, u32[]{:S(2)}, u32[]{:S(2)}) async-start(bf16[8,16,2048]{2,1,0:T(8,128)(2,1)} %bitcast.384), calls=%async_computation.2 | async-start | bytes 1048576 | tf_op jit(solution)/shard_map/all_to_all | solution.py:47
  36.7 17.4 %all-to-all-start = ((bf16[8,16,2048]{2,1,0:T(8,128)(2,1)}), bf16[8,16,2048]{2,1,0:T(8,128)(2,1)S(1)}, u32[]{:S(2)}, u32[]{:S(2)}) async-start(bf16[8,16,2048]{2,1,0:T(8,128)(2,1)} %bitcast.19), calls=%async_computation | async-start | bytes 1048576 | tf_op jit(solution)/shard_map/all_to_all | solution.py:47
  54.1 17.4 %all-to-all-start.6 = ((bf16[8,16,2048]{2,1,0:T(8,128)(2,1)}), bf16[8,16,2048]{2,1,0:T(8,128)(2,1)S(1)}, u32[]{:S(2)}, u32[]{:S(2)}) async-start(bf16[8,16,2048]{2,1,0:T(8,128)(2,1)} %bitcast.64), calls=%async_computation.6 | async-start | bytes 1048576 | tf_op jit(solution)/shard_map/all_to_all | solution.py:47
  89.5 95.4 %all-to-all-start.3 = ((f32[4,8,16,2048]{3,2,0,1:T(8,128)}), f32[4,8,16,2048]{3,2,0,1:T(8,128)}, u32[]{:S(2)}, u32[]{:S(2)}) async-start(f32[4,8,16,2048]{3,2,0,1:T(8,128)} %pad_maximum_fusion.1), calls=%async_computation.3 | async-start | bytes 8388608 | tf_op jit(solution)/shard_map/all_to_all | solution.py:79
  99.4 92.5 %copy-start.23 = (f32[1,8,16,2048]{3,2,0,1:T(8,128)S(1)}, f32[1,8,16,2048]{3,2,0,1:T(8,128)}, u32[]{:S(2)}) copy-start(f32[1,8,16,2048]{3,2,0,1:T(8,128)} %get-tuple-element.70) | copy-start | bytes 3145732
  99.4 92.5 %copy-start.31 = (f32[1,8,16,2048]{3,2,0,1:T(8,128)S(1)}, f32[1,8,16,2048]{3,2,0,1:T(8,128)}, u32[]{:S(2)}) copy-start(f32[1,8,16,2048]{3,2,0,1:T(8,128)} %get-tuple-element.71) | copy-start | bytes 3145732
  184.9 97.1 %all-to-all-start.1 = ((f32[4,8,16,2048]{3,2,0,1:T(8,128)}), f32[4,8,16,2048]{3,2,0,1:T(8,128)}, u32[]{:S(2)}, u32[]{:S(2)}) async-start(f32[4,8,16,2048]{3,2,0,1:T(8,128)} %pad_maximum_fusion), calls=%async_computation.1 | async-start | bytes 8388608 | tf_op jit(solution)/shard_map/all_to_all | solution.py:79
  281.9 97.1 %all-to-all-start.7 = ((f32[4,8,16,2048]{3,2,0,1:T(8,128)}), f32[4,8,16,2048]{3,2,0,1:T(8,128)}, u32[]{:S(2)}, u32[]{:S(2)}) async-start(f32[4,8,16,2048]{3,2,0,1:T(8,128)} %pad_maximum_fusion.3), calls=%async_computation.7 | async-start | bytes 8388608 | tf_op jit(solution)/shard_map/all_to_all | solution.py:79
  442.1 52.5 %all-to-all-start.4 = ((bf16[4,8,16,2048]{3,2,0,1:T(8,128)(2,1)}), bf16[4,8,16,2048]{3,2,0,1:T(8,128)(2,1)S(1)}, u32[]{:S(2)}, u32[]{:S(2)}) async-start(bf16[4,8,16,2048]{3,2,0,1:T(8,128)(2,1)} %pad_maximum_fusion.8), calls=%async_computation.4 | async-start | bytes 4194304 | tf_op jit(solution)/shard_map/all_to_all | solution.py:103
  496.0 52.1 %all-to-all-start.8 = ((bf16[4,8,16,2048]{3,2,0,1:T(8,128)(2,1)}), bf16[4,8,16,2048]{3,2,0,1:T(8,128)(2,1)S(1)}, u32[]{:S(2)}, u32[]{:S(2)}) async-start(bf16[4,8,16,2048]{3,2,0,1:T(8,128)(2,1)} %pad_maximum_fusion.11), calls=%async_computation.8 | async-start | bytes 4194304 | tf_op jit(solution)/shard_map/all_to_all | solution.py:103
  549.4 52.1 %all-to-all-start.10 = ((bf16[4,8,16,2048]{3,2,0,1:T(8,128)(2,1)}), bf16[4,8,16,2048]{3,2,0,1:T(8,128)(2,1)S(1)}, u32[]{:S(2)}, u32[]{:S(2)}) async-start(bf16[4,8,16,2048]{3,2,0,1:T(8,128)(2,1)} %pad_maximum_fusion.14), calls=%async_computation.10 | async-start | bytes 4194304 | tf_op jit(solution)/shard_map/all_to_all | solution.py:103
  601.4 29.7 %all-to-all-start.5 = ((f32[8,16,2048]{2,1,0:T(8,128)}), f32[8,16,2048]{2,1,0:T(8,128)S(1)}, u32[]{:S(2)}, u32[]{:S(2)}) async-start(f32[8,16,2048]{2,1,0:T(8,128)} %copy.115), calls=%async_computation.5 | async-start | bytes 2097152 | tf_op jit(solution)/shard_map/all_to_all | solution.py:51
  632.1 29.6 %all-to-all-start.9 = ((f32[8,16,2048]{2,1,0:T(8,128)}), f32[8,16,2048]{2,1,0:T(8,128)S(1)}, u32[]{:S(2)}, u32[]{:S(2)}) async-start(f32[8,16,2048]{2,1,0:T(8,128)} %copy.122), calls=%async_computation.9 | async-start | bytes 2097152 | tf_op jit(solution)/shard_map/all_to_all | solution.py:51
  661.6 81.8 %all-to-all-start.11 = ((bf16[8,16,2048]{2,1,0:T(8,128)(2,1)}), bf16[8,16,2048]{2,1,0:T(8,128)(2,1)}, u32[]{:S(2)}, u32[]{:S(2)}) async-start(bf16[8,16,2048]{2,1,0:T(8,128)(2,1)} %copy.124), calls=%async_computation.11 | async-start | bytes 1048576 | tf_op jit(solution)/shard_map/all_to_all | solution.py:51
  668.1 74.7 %all-reduce.3.cloned.1.call-start = ((), (), s32[]{:S(2)}) async-start(), calls=%async_computation.14 | async-start | bytes 196608 | tf_op jit(solution)/shard_map/psum | solution.py:256
  668.4 82.6 %copy-start.56 = (f32[1,1,2048]{2,1,0:T(1,128)S(1)}, f32[1,1,2048]{2,1,0:T(1,128)}, u32[]{:S(2)}) copy-start(f32[1,1,2048]{2,1,0:T(1,128)} %copy-done.55) | copy-start | bytes 24580
  673.0 103.2 %all-reduce.5.cloned.1.call-start = ((), (), s32[]{:S(2)}) async-start(), calls=%async_computation.15 | async-start | bytes 196608 | tf_op jit(solution)/shard_map/psum | solution.py:256
  698.7 52.2 %collective-permute-start.3 = (f32[2,2048]{1,0:T(2,128)S(1)}, f32[2,2048]{1,0:T(2,128)S(1)}, u32[]{:S(2)}, u32[]{:S(2)}) collective-permute-start(f32[2,2048]{1,0:T(2,128)S(1)} %slice.390), channel_id=1, source_target_pairs={{1,0},{2,1},{3,2},{4,3},{5,4},{6,5},{7,6},{9,8},{10,9},{11,10},{12... | collective-permute-start | bytes 49160 | tf_op jit(solution)/shard_map/ppermute | solution.py:10
  742.8 57.7 %reduce-scatter.2.cloned.1.call-start = ((), (), s32[]{:S(2)}) async-start(), calls=%async_computation.13 | async-start | bytes 655360 | tf_op jit(solution)/shard_map/reduce_scatter | solution.py:235
  744.4 10.0 %collective-permute-start.4 = (f32[2,2048]{1,0:T(2,128)S(1)}, f32[2,2048]{1,0:T(2,128)S(1)}, u32[]{:S(2)}, u32[]{:S(2)}) collective-permute-start(f32[2,2048]{1,0:T(2,128)S(1)} %slice.406), channel_id=1, source_target_pairs={{1,0},{2,1},{3,2},{4,3},{5,4},{6,5},{7,6},{9,8},{10,9},{11,10},{12... | collective-permute-start | bytes 49160 | tf_op jit(solution)/shard_map/ppermute | solution.py:10
  747.8 6.6 collective-permute-start.5
  (66 other events, 1091.6 us)
Sparse Core Ops, SparseCore 0:
  673.2 69.5 all-reduce.2
  745.1 31.0 all-reduce.4
  778.8 21.6 reduce-scatter.1
